TPU v7x, 512 devices: a whole 4x4x16 slice. The times are simulated.
512 devices in a mesh: sample: 32 (over y, x, core), space: 16 (over z).
Axes of the slice: x: 4, y: 4, z: 16, core: 2. Of those that a mesh axis runs over, the one named last changes fastest.
Arguments:
- volumes: bfloat16 [32, 32, 64, 16, 128], P('sample', None, 'space'), may hold values from -360 to 360
- depth_kernel: float32 [32, 27], replicated, may hold values from -1.25 to 1.25
- point_weight: bfloat16 [32, 32], replicated, may hold values from -1 to 1
- cotangent: bfloat16 [32, 32, 64, 16, 128], P('sample', None, 'space'), may hold values from -4.1 to 4.1
Outputs:
- whitened: bfloat16 [32, 32, 64, 16, 128], P('sample', None, 'space')
- d_volumes: bfloat16 [32, 32, 64, 16, 128], P('sample', None, 'space')
- d_point: float32 [32, 32], replicated
- d_kernel: float32 [32, 27], replicated
All inputs are finite; a program needn't handle non-finite values.
Results may differ from a plain program's by a relative error of at most 0.0067.
Values may be sent and summed in bfloat16 or wider, within the bound.
No kernel may reach another device: no remote copies, remote signals or barrier semaphores. Data moves between devices by JAX's collectives and lax.ppermute only.
A program may use at most 64 MiB of HBM per device.

v0:
```python
from functools import partial
import math
import jax
import jax.numpy as jnp
from jax import lax
from jax.sharding import PartitionSpec as P

GSIZE = 16
NEWTON = 5
GROUPS = 2
epsilon = 1e-05
highest = lax.Precision.HIGHEST


def with_halo(block, sides, width):
    for axis, dim in sides:
        count = lax.axis_size(axis)
        forward = [(i, i + 1) for i in range(count - 1)]
        backward = [(target, source) for source, target in forward]
        low = lax.ppermute(
            lax.slice_in_dim(block, block.shape[dim] - width, None, axis=dim), axis, forward
        )
        high = lax.ppermute(lax.slice_in_dim(block, 0, width, axis=dim), axis, backward)
        block = jnp.concatenate([low, block, high], axis=dim)
    return block


def matmul_high(matrix, operand):
    return jnp.matmul(matrix, operand, precision=highest)


def contract_rows(matrix, operand):
    return jnp.einsum(
        "cv,dv->cd", matrix, operand, precision=highest, preferred_element_type=jnp.float32
    )


def contract_cols(matrix, operand):
    return jnp.einsum(
        "kc,kv->cv", matrix, operand, precision=highest, preferred_element_type=jnp.float32
    )


def block_diagonal(blocks):
    identity = jnp.eye(blocks.shape[0], dtype=blocks.dtype)
    full_size = blocks.shape[0] * blocks.shape[1]
    return jnp.einsum("gh,gij->gihj", identity, blocks, precision=highest).reshape(
        full_size, full_size
    )


def whiten_stats(first_sums, second_sums, voxel_count):
    groups = second_sums.shape[0]
    group_size = second_sums.shape[1]
    average = (first_sums / voxel_count).reshape(groups, group_size)
    identity = jnp.eye(group_size, dtype=second_sums.dtype)
    covariance = (
        second_sums / voxel_count - average[:, :, None] * average[:, None, :] + epsilon * identity
    )
    traces = jnp.trace(covariance, axis1=1, axis2=2)
    normed = covariance / traces[:, None, None]
    project = jnp.broadcast_to(identity, covariance.shape)
    for newton_step in range(NEWTON):
        cubed = matmul_high(matmul_high(project, project), project)
        project = 0.5 * (3.0 * project - matmul_high(cubed, normed))
    whiten_mat = project / jnp.sqrt(traces)[:, None, None]
    offset = jnp.einsum("gij,gj->gi", whiten_mat, average, precision=highest)
    return (whiten_mat, offset)


def adjoint_terms(pull_back, whiten_mat, grad_first, grad_second):
    d_first, d_second = pull_back(
        (grad_second, -grad_first.reshape(whiten_mat.shape[0], whiten_mat.shape[1]))
    )
    adjoint = block_diagonal(jnp.swapaxes(whiten_mat, 1, 2))
    symmetric = block_diagonal(d_second + jnp.swapaxes(d_second, 1, 2))
    return (d_first, adjoint, symmetric)


def gradient_signal(adjoint, d_first, symmetric, grad_part, mixed_part):
    first_term = jnp.dot(adjoint, grad_part, precision=highest, preferred_element_type=jnp.float32)
    third_term = jnp.dot(
        symmetric, mixed_part, precision=highest, preferred_element_type=jnp.float32
    )
    return first_term + d_first[:, None] + third_term


def pad_sides(extended):
    return jnp.pad(extended, ((0, 0), (0, 0), (1, 1), (1, 1)))


def tap_cells(padded, tap_index, depth_cells):
    plane_off = tap_index // 9
    row_off = tap_index // 3 % 3
    col_off = tap_index % 3
    height = padded.shape[2] - 2
    width_cells = padded.shape[3] - 2
    return padded[
        :,
        plane_off : plane_off + depth_cells,
        row_off : row_off + height,
        col_off : col_off + width_cells,
    ]


def depth_conv(extended, kernel, depth_cells):
    padded = pad_sides(extended)
    summed = jnp.zeros(
        (extended.shape[0], depth_cells, extended.shape[2], extended.shape[3]), jnp.float32
    )
    for tap_index in range(27):
        summed = summed + kernel[:, tap_index][:, None, None, None] * tap_cells(
            padded, tap_index, depth_cells
        ).astype(jnp.float32)
    return summed


def depth_adjoint(grad_ext, kernel, depth_cells):
    padded = pad_sides(grad_ext)
    height = grad_ext.shape[2]
    width_cells = grad_ext.shape[3]
    summed = jnp.zeros((grad_ext.shape[0], depth_cells, height, width_cells), jnp.float32)
    for tap_index in range(27):
        plane_off = 2 - tap_index // 9
        row_off = 2 - tap_index // 3 % 3
        col_off = 2 - tap_index % 3
        summed = (
            summed
            + kernel[:, tap_index][:, None, None, None]
            * padded[
                :,
                plane_off : plane_off + depth_cells,
                row_off : row_off + height,
                col_off : col_off + width_cells,
            ]
        )
    return summed


def on_device(volumes, depth_kernel, point_weight, cotangent):
    volume = volumes[0]
    grad_in = cotangent[0]
    channels, depth_cells, height, width_cells = volume.shape
    voxels = depth_cells * height * width_cells
    voxel_count = float(voxels * lax.axis_size("sample") * lax.axis_size("space"))
    grad_flat = grad_in.reshape(channels, voxels)
    extended = with_halo(volume, (("space", 1),), 1)
    hidden = (
        depth_conv(extended, depth_kernel, depth_cells)
        .astype(jnp.bfloat16)
        .reshape(channels, voxels)
    )
    mixed_out = jnp.dot(point_weight, hidden, preferred_element_type=jnp.float32).astype(
        jnp.bfloat16
    )
    grouped = mixed_out.reshape(GROUPS, GSIZE, voxels)
    local_first = jnp.sum(mixed_out.astype(jnp.float32), axis=1)
    local_second = jnp.einsum("giv,gjv->gij", grouped, grouped, preferred_element_type=jnp.float32)
    grad_first = jnp.sum(grad_flat.astype(jnp.float32), axis=1)
    grad_second = jnp.einsum(
        "giv,gjv->gij",
        grad_flat.reshape(GROUPS, GSIZE, voxels),
        grouped,
        preferred_element_type=jnp.float32,
    )
    padded_x = pad_sides(extended)
    weight_f = point_weight.astype(jnp.float32)
    stats_fn = partial(whiten_stats, voxel_count=voxel_count)
    first_sums, second_sums, grad_first, grad_second = lax.psum(
        (local_first, local_second, grad_first, grad_second), ("sample", "space")
    )
    (whiten_mat, offset), pull_back = jax.vjp(stats_fn, first_sums, second_sums)
    d_first, adjoint, symmetric = adjoint_terms(pull_back, whiten_mat, grad_first, grad_second)
    whitened = (
        jnp.dot(
            block_diagonal(whiten_mat),
            mixed_out,
            precision=highest,
            preferred_element_type=jnp.float32,
        )
        - offset.reshape(channels)[:, None]
    ).astype(jnp.bfloat16)
    d_mixed = gradient_signal(adjoint, d_first, symmetric, grad_flat, mixed_out)
    d_hidden = contract_cols(weight_f, d_mixed).reshape(channels, depth_cells, height, width_cells)
    grad_ext = with_halo(d_hidden, (("space", 1),), 1)
    kernel_terms = jnp.stack(
        [
            jnp.sum(
                d_hidden * tap_cells(padded_x, tap_index, depth_cells).astype(jnp.float32),
                axis=(1, 2, 3),
            )
            for tap_index in range(27)
        ],
        axis=1,
    )
    d_point, d_kernel = lax.psum(
        (contract_rows(d_mixed, hidden), kernel_terms), ("sample", "space")
    )
    d_volume = depth_adjoint(grad_ext, depth_kernel, depth_cells).astype(jnp.bfloat16)
    scale_out = 1.0 / math.sqrt(voxel_count)
    return (
        whitened.reshape(1, channels, depth_cells, height, width_cells),
        d_volume[None],
        d_point * scale_out,
        d_kernel * scale_out,
    )


def solution(mesh):
    in_specs = (
        P("sample", None, "space", None, None),
        P(),
        P(),
        P("sample", None, "space", None, None),
    )
    out_specs = (
        P("sample", None, "space", None, None),
        P("sample", None, "space", None, None),
        P(),
        P(),
    )
    return jax.shard_map(
        on_device, mesh=mesh, in_specs=in_specs, out_specs=out_specs, check_vma=False
    )
```

profile of v0, /device:TPU:1, one launch (start us, length us, event | category | flops | bytes accessed | tf_op | source)
XLA Modules:
  0.0 388.2 jit_solution(1286581559153312555)
XLA Ops:
  1.8 4.4 %collective-permute-start = (bf16[32,1,16,128]{3,2,1,0:T(8,128)(2,1)S(1)}, bf16[32,1,16,128]{3,2,1,0:T(8,128)(2,1)S(1)}, u32[]{:S(2)}, u32[]{:S(2)}) collective-permute-start(bf16[32,1,16,128]{3,2,1,0:T(8,128)(2,1)S(1)} %get-tuple-element.77), channel_id=1, source_target_pairs={{0,1},{1,2},{2,3},{3,4},{4,5},{5,6},{6,7},{7,8},{8,9},{9,10},{10,1... | collective-permute-start | bytes 393224 | tf_op jit(solution)/shard_map/ppermute | solution.py:20
  9.2 1.9 slice_reduce_fusion.25
  11.1 2.6 slice_reduce_fusion.26
  13.7 2.1 reshape_squeeze.3
  15.8 2.1 reshape_reshape_squeeze.3
  17.8 2.2 reshape.120
  22.5 3.0 select_maximum_fusion.2
  25.5 7.8 %fusion.59 = bf16[32,4,16,128]{3,2,1,0:T(8,128)(2,1)S(1)} fusion(bf16[32,4,16,128]{3,2,1,0:T(8,128)(2,1)S(1)} %bitcast.174, bf16[32,1,16,128]{3,2,1,0:T(8,128)(2,1)} %collective-permute-done.1, bf16[32,1,16,128]{3,2,1,0:T(8,128)(2,1)S(1)} %collective-permute-done, f32[32]{0:T(128)} %get-tuple-element.67, f32[32]{0:T(128)} %get-tuple-element.68, ...), kind=kLoop, calls=%fused_computation.140 | loop fusion | flops 21757952 | bytes 13897088 | tf_op jit(solution)/shard_map/convert_element_type | solution.py:150
  36.4 111.9 %all-reduce.3 = (f32[32]{0:T(128)}, f32[2,16,16]{2,1,0:T(8,128)}, f32[2,16,16]{1,2,0:T(8,128)}, f32[32]{0:T(128)}) all-reduce(f32[32]{0:T(128)} %get-tuple-element.91, f32[2,16,16]{2,1,0:T(8,128)} %fusion.215, f32[2,16,16]{1,2,0:T(8,128)} %convolution_bitcast_fusion, ...), channel_id=1, replica_groups=mesh['sample'=32,'space'=16] {'sample','space'}, use_global_device_ids=true, to_apply=%region_2.3 | all-reduce | flops 1088 | bytes 8704 | tf_op jit(solution)/shard_map/psum | solution.py:169
  162.7 1.6 fusion.212
  168.7 1.5 fusion.211
  174.2 1.5 fusion.210
  179.6 1.5 fusion.209
  198.2 1.6 fusion.208
  205.4 1.6 multiply_reduce_fusion.2
  209.7 1.5 multiply_reduce_fusion.3
  214.2 1.4 multiply_reduce_fusion.1
  218.5 1.5 multiply_bitcast_fusion
  220.0 1.4 reshape.118
  221.4 1.4 reshape.117
  222.9 1.7 convolution_add_fusion.1
  225.9 1.5 fusion.91
  228.9 6.7 %fusion.60 = (f32[32]{0:T(128)S(1)}, f32[32]{0:T(128)S(1)}, f32[32]{0:T(128)}, f32[32]{0:T(128)}, f32[32]{0:T(128)}, /*index=5*/f32[32]{0:T(128)}, f32[32]{0:T(1...) fusion(f32[32,4,16,128]{3,2,1,0:T(8,128)S(1)} %bitcast.164, ...), kind=kLoop, calls=%fused_computation.141 | loop fusion | flops 14155200 | bytes 10488064 | tf_op jit(solution)/shard_map/reduce_sum | solution.py:188
  238.4 1.4 reshape.115
  239.8 4.3 %fusion.57 = (f32[32]{0:T(128)}, f32[32]{0:T(128)}, f32[32]{0:T(128)}, f32[32]{0:T(128)}, f32[32]{0:T(128)}, /*index=5*/f32[32]{0:T(128)}, f32[32]{0:T(128)}, f32[32]{0:T(128)}) fusion(f32[32,4,16,128]{3,2,1,0:T(8,128)S(1)} %bitcast.166, bf16[32,6,18,130]{3,2,1,0:T(8,128)(2,1)S(1)} %select_maximum_fusion.2, bf16[32,4,16,128]{3,2,1,0:T(8,128)(2,1)} %bitcast.172, ...), kind=kLoop, calls=%fused_computation.138 | loop fusion | flops 6815488 | bytes 4981760 | tf_op jit(solution)/shard_map/reduce_sum | solution.py:188
  244.4 2.8 stack.111
  247.2 99.9 %all-reduce.2 = (f32[32,32]{1,0:T(8,128)S(1)}, f32[32,27]{0,1:T(8,128)S(1)}) all-reduce(f32[32,32]{1,0:T(8,128)} %fusion.91, f32[32,27]{0,1:T(8,128)S(1)} %stack.111), channel_id=1, replica_groups=mesh['sample'=32,'space'=16] {'sample','space'}, use_global_device_ids=true, to_apply=%region_11.12 | all-reduce | flops 1888 | bytes 15104 | tf_op jit(solution)/shard_map/psum | solution.py:196
  347.1 3.3 collective-permute-start.2
  351.6 1.6 fusion.5
  355.6 3.7 collective-permute-done.3
  359.3 3.4 select_maximum_fusion
  363.0 25.1 %fusion.94 = bf16[1,32,4,16,128]{4,3,2,1,0:T(8,128)(2,1)} fusion(f32[32,6,18,130]{3,2,1,0:T(8,128)} %select_maximum_fusion, f32[32]{0:T(128)S(1)} %copy-done.23, f32[32]{0:T(128)S(1)} %copy-done.24, f32[32]{0:T(128)S(1)} %copy-done.26, f32[32]{0:T(128)S(1)} %copy-done.27, f32[32,4,16,128]{3,2,1,0:T(8,128)S(1)} %bitcast.168, ...), kind=kLoop, calls=%fused_computation.206 | loop fusion | flops 14680064 | bytes 27266432 | tf_op jit(solution)/shard_map/broadcast_in_dim | solution.py:203
  (180 shorter events, 76.9 us)
Async XLA Ops:
  1.8 20.8 %collective-permute-start = (bf16[32,1,16,128]{3,2,1,0:T(8,128)(2,1)S(1)}, bf16[32,1,16,128]{3,2,1,0:T(8,128)(2,1)S(1)}, u32[]{:S(2)}, u32[]{:S(2)}) collective-permute-start(bf16[32,1,16,128]{3,2,1,0:T(8,128)(2,1)S(1)} %get-tuple-element.77), channel_id=1, source_target_pairs={{0,1},{1,2},{2,3},{3,4},{4,5},{5,6},{6,7},{7,8},{8,9},{9,10},{10,1... | collective-permute-start | bytes 393224 | tf_op jit(solution)/shard_map/ppermute | solution.py:20
  6.1 16.4 %collective-permute-start.1 = (bf16[32,1,16,128]{3,2,1,0:T(8,128)(2,1)S(1)}, bf16[32,1,16,128]{3,2,1,0:T(8,128)(2,1)}, u32[]{:S(2)}, u32[]{:S(2)}) collective-permute-start(bf16[32,1,16,128]{3,2,1,0:T(8,128)(2,1)S(1)} %get-tuple-element.78), channel_id=1, source_target_pairs={{1,0},{2,1},{3,2},{4,3},{5,4},{6,5},{7,6},{8,7},{9,8},{10,9},{11,1... | collective-permute-start | bytes 393224 | tf_op jit(solution)/shard_map/ppermute | solution.py:23
  34.5 191.4 %copy-start.1 = (bf16[8192,32]{0,1:T(8,128)(2,1)}, bf16[8192,32]{0,1:T(8,128)(2,1)S(1)}, u32[]{:S(2)}) copy-start(bf16[8192,32]{0,1:T(8,128)(2,1)S(1)} %get-tuple-element.92) | copy-start | bytes 1572868
  244.2 118.6 %copy-start.17 = (f32[32]{0:T(128)S(1)}, f32[32]{0:T(128)}, u32[]{:S(2)}) copy-start(f32[32]{0:T(128)} %get-tuple-element.61) | copy-start | bytes 388
  244.2 118.6 %copy-start.18 = (f32[32]{0:T(128)S(1)}, f32[32]{0:T(128)}, u32[]{:S(2)}) copy-start(f32[32]{0:T(128)} %get-tuple-element.62) | copy-start | bytes 388
  244.2 118.6 %copy-start.19 = (f32[32]{0:T(128)S(1)}, f32[32]{0:T(128)}, u32[]{:S(2)}) copy-start(f32[32]{0:T(128)} %get-tuple-element.63) | copy-start | bytes 388
  244.2 118.6 %copy-start.20 = (f32[32]{0:T(128)S(1)}, f32[32]{0:T(128)}, u32[]{:S(2)}) copy-start(f32[32]{0:T(128)} %get-tuple-element.64) | copy-start | bytes 388
  244.2 118.6 %copy-start.21 = (f32[32]{0:T(128)S(1)}, f32[32]{0:T(128)}, u32[]{:S(2)}) copy-start(f32[32]{0:T(128)} %get-tuple-element.65) | copy-start | bytes 388
  244.2 118.6 %copy-start.22 = (f32[32]{0:T(128)S(1)}, f32[32]{0:T(128)}, u32[]{:S(2)}) copy-start(f32[32]{0:T(128)} %get-tuple-element.66) | copy-start | bytes 388
  244.2 118.6 %copy-start.23 = (f32[32]{0:T(128)S(1)}, f32[32]{0:T(128)}, u32[]{:S(2)}) copy-start(f32[32]{0:T(128)} %get-tuple-element.67) | copy-start | bytes 388
  244.2 118.6 %copy-start.24 = (f32[32]{0:T(128)S(1)}, f32[32]{0:T(128)}, u32[]{:S(2)}) copy-start(f32[32]{0:T(128)} %get-tuple-element.68) | copy-start | bytes 388
  244.2 118.6 %copy-start.25 = (f32[32]{0:T(128)S(1)}, f32[32]{0:T(128)}, u32[]{:S(2)}) copy-start(f32[32]{0:T(128)} %get-tuple-element.42) | copy-start | bytes 388
  244.2 118.6 %copy-start.26 = (f32[32]{0:T(128)S(1)}, f32[32]{0:T(128)}, u32[]{:S(2)}) copy-start(f32[32]{0:T(128)} %get-tuple-element.43) | copy-start | bytes 388
  244.2 118.6 %copy-start.27 = (f32[32]{0:T(128)S(1)}, f32[32]{0:T(128)}, u32[]{:S(2)}) copy-start(f32[32]{0:T(128)} %get-tuple-element.44) | copy-start | bytes 388
  244.2 118.6 %copy-start.28 = (f32[32]{0:T(128)S(1)}, f32[32]{0:T(128)}, u32[]{:S(2)}) copy-start(f32[32]{0:T(128)} %get-tuple-element.45) | copy-start | bytes 388
  244.3 118.6 %copy-start.29 = (f32[32]{0:T(128)S(1)}, f32[32]{0:T(128)}, u32[]{:S(2)}) copy-start(f32[32]{0:T(128)} %get-tuple-element.46) | copy-start | bytes 388
  244.3 118.6 %copy-start.30 = (f32[32]{0:T(128)S(1)}, f32[32]{0:T(128)}, u32[]{:S(2)}) copy-start(f32[32]{0:T(128)} %get-tuple-element.47) | copy-start | bytes 388
  244.3 118.6 %copy-start.31 = (f32[32]{0:T(128)S(1)}, f32[32]{0:T(128)}, u32[]{:S(2)}) copy-start(f32[32]{0:T(128)} %get-tuple-element.48) | copy-start | bytes 388
  244.3 118.6 %copy-start.32 = (f32[32]{0:T(128)S(1)}, f32[32]{0:T(128)}, u32[]{:S(2)}) copy-start(f32[32]{0:T(128)} %get-tuple-element.49) | copy-start | bytes 388
  244.3 118.6 %copy-start.33 = (f32[32]{0:T(128)S(1)}, f32[32]{0:T(128)}, u32[]{:S(2)}) copy-start(f32[32]{0:T(128)} %get-tuple-element.50) | copy-start | bytes 388
  244.3 118.6 %copy-start.34 = (f32[32]{0:T(128)S(1)}, f32[32]{0:T(128)}, u32[]{:S(2)}) copy-start(f32[32]{0:T(128)} %get-tuple-element.51) | copy-start | bytes 388
  244.3 118.6 %copy-start.35 = (f32[32]{0:T(128)S(1)}, f32[32]{0:T(128)}, u32[]{:S(2)}) copy-start(f32[32]{0:T(128)} %get-tuple-element.52) | copy-start | bytes 388
  244.3 118.6 %copy-start.36 = (f32[32]{0:T(128)S(1)}, f32[32]{0:T(128)}, u32[]{:S(2)}) copy-start(f32[32]{0:T(128)} %get-tuple-element.53) | copy-start | bytes 388
  244.3 118.6 %copy-start.37 = (f32[32]{0:T(128)S(1)}, f32[32]{0:T(128)}, u32[]{:S(2)}) copy-start(f32[32]{0:T(128)} %get-tuple-element.54) | copy-start | bytes 388
  244.3 118.6 %copy-start.38 = (f32[32]{0:T(128)S(1)}, f32[32]{0:T(128)}, u32[]{:S(2)}) copy-start(f32[32]{0:T(128)} %get-tuple-element.55) | copy-start | bytes 388
  244.4 118.6 %copy-start.39 = (f32[32]{0:T(128)S(1)}, f32[32]{0:T(128)}, u32[]{:S(2)}) copy-start(f32[32]{0:T(128)} %get-tuple-element.56) | copy-start | bytes 388
  244.4 118.6 %copy-start.40 = (f32[32]{0:T(128)S(1)}, f32[32]{0:T(128)}, u32[]{:S(2)}) copy-start(f32[32]{0:T(128)} %get-tuple-element.57) | copy-start | bytes 388
  244.4 118.6 %copy-start.41 = (f32[32]{0:T(128)S(1)}, f32[32]{0:T(128)}, u32[]{:S(2)}) copy-start(f32[32]{0:T(128)} %get-tuple-element.58) | copy-start | bytes 388
  244.4 118.6 %copy-start.42 = (f32[32]{0:T(128)S(1)}, f32[32]{0:T(128)}, u32[]{:S(2)}) copy-start(f32[32]{0:T(128)} %get-tuple-element.59) | copy-start | bytes 388
  244.4 118.6 %copy-start.43 = (f32[32]{0:T(128)S(1)}, f32[32]{0:T(128)}, u32[]{:S(2)}) copy-start(f32[32]{0:T(128)} %get-tuple-element.60) | copy-start | bytes 388
  347.1 8.5 %collective-permute-start.2 = (f32[32,1,16,128]{3,2,1,0:T(8,128)}, f32[32,1,16,128]{3,2,1,0:T(8,128)S(1)}, u32[]{:S(2)}, u32[]{:S(2)}) collective-permute-start(f32[32,1,16,128]{3,2,1,0:T(8,128)} %get-tuple-element.75), channel_id=1, source_target_pairs={{0,1},{1,2},{2,3},{3,4},{4,5},{5,6},{6,7},{7,8},{8,9},{9,10},{10,1... | collective-permute-start | bytes 786440 | tf_op jit(solution)/shard_map/ppermute | solution.py:20
  350.3 9.0 %collective-permute-start.3 = (f32[32,1,16,128]{3,2,1,0:T(8,128)}, f32[32,1,16,128]{3,2,1,0:T(8,128)S(1)}, u32[]{:S(2)}, u32[]{:S(2)}) collective-permute-start(f32[32,1,16,128]{3,2,1,0:T(8,128)} %get-tuple-element.76), channel_id=1, source_target_pairs={{1,0},{2,1},{3,2},{4,3},{5,4},{6,5},{7,6},{8,7},{9,8},{10,9},{11,1... | collective-permute-start | bytes 786440 | tf_op jit(solution)/shard_map/ppermute | solution.py:23
  (17 other events, 113.1 us)
where the time goes:
time: 394 us; the launch traced here: 388 us
  blocking collectives  212 us (54%)
  other arithmetic  67.2 us (17%)
  local copies, waits for them, and re-layouts  48.5 us (12%)
  matrix products  45.2 us (11%)
  starting transfers between devices  10.2 us (3%)
    psum x1, blocking collectives, on_device(): lax.psum((local_first, local_second, grad_first, grad_second), ('sample',...  112 us
    psum x1, blocking collectives, on_device(): lax.psum((contract_rows(d_mixed, hidden), kernel_terms), ('sample', 'spac...  99.9 us
    dot_general x40, matrix products, matmul_high(): return jnp.matmul(matrix, operand, precision=highest)  33.2 us
    broadcast_in_dim x1, other arithmetic, on_device(): d_volume[None]  25.1 us
    reduce_sum x2, other arithmetic, on_device(): jnp.sum(d_hidden * tap_cells(padded_x, tap_index, depth_cells).astype(jnp...  11 us
  transfers between devices with their start and end apart: 4, of which 2 were waited for; matrix products, arithmetic and copies ran while one was open for 5% of the time, Pallas kernels for 0%

commit v1 on v0

--- a/solution.py
+++ b/solution.py
@@ -10,6 +10,10 @@
 GROUPS = 2
 epsilon = 1e-05
 highest = lax.Precision.HIGHEST
+
+
+def records_order(xin, a_name, mesh_name):
+    return lax.psum(lax.psum(xin, a_name), mesh_name)
 
 
 def with_halo(block, sides, width):
@@ -193,8 +197,8 @@
         ],
         axis=1,
     )
-    d_point, d_kernel = lax.psum(
-        (contract_rows(d_mixed, hidden), kernel_terms), ("sample", "space")
+    d_point, d_kernel = records_order(
+        (contract_rows(d_mixed, hidden), kernel_terms), "sample", "space"
     )
     d_volume = depth_adjoint(grad_ext, depth_kernel, depth_cells).astype(jnp.bfloat16)
     scale_out = 1.0 / math.sqrt(voxel_count)

time: 394 us -> 470 us (1.19)
  the two profiles are of different devices: /device:TPU:1 before, /device:TPU:96 now
where the time goes in v1:
time: 470 us; the launch traced here: 464 us
  blocking collectives  283 us (60%)
  other arithmetic  67.2 us (14%)
  local copies, waits for them, and re-layouts  48.5 us (10%)
  matrix products  45.2 us (10%)
  starting transfers between devices  14.3 us (3%)
    psum x2, blocking collectives, records_order(): return lax.psum(lax.psum(xin, a_name), mesh_name)  177 us
    psum x1, blocking collectives, on_device(): lax.psum((local_first, local_second, grad_first, grad_second), ('sample',...  107 us
    dot_general x40, matrix products, matmul_high(): return jnp.matmul(matrix, operand, precision=highest)  33.2 us
    broadcast_in_dim x1, other arithmetic, on_device(): d_volume[None]  25.1 us
    reduce_sum x2, other arithmetic, on_device(): jnp.sum(d_hidden * tap_cells(padded_x, tap_index, depth_cells).astype(jnp...  11 us
    ppermute x2, starting transfers between devices, with_halo(): lax.ppermute(lax.slice_in_dim(block, block.shape[dim] - width, None, axis...  10.4 us
  transfers between devices with their start and end apart: 4, of which 1 were waited for; matrix products, arithmetic and copies ran while one was open for 4% of the time, Pallas kernels for 0%

profile of v1, /device:TPU:96, one launch (start us, length us, event | category | flops | bytes accessed | tf_op | source)
XLA Modules:
  0.0 464.0 jit_solution(16114698769366652999)
XLA Ops:
  1.8 5.0 %collective-permute-start = (bf16[32,1,16,128]{3,2,1,0:T(8,128)(2,1)S(1)}, bf16[32,1,16,128]{3,2,1,0:T(8,128)(2,1)S(1)}, u32[]{:S(2)}, u32[]{:S(2)}) collective-permute-start(bf16[32,1,16,128]{3,2,1,0:T(8,128)(2,1)S(1)} %get-tuple-element.79), channel_id=1, source_target_pairs={{0,1},{1,2},{2,3},{3,4},{4,5},{5,6},{6,7},{7,8},{8,9},{9,10},{10,1... | collective-permute-start | bytes 393224 | tf_op jit(solution)/shard_map/ppermute | solution.py:24
  6.8 1.9 collective-permute-start.1
  10.5 1.9 slice_reduce_fusion.25
  12.4 2.6 slice_reduce_fusion.26
  15.0 2.1 reshape_squeeze.3
  17.1 2.1 reshape_reshape_squeeze.3
  19.1 2.2 reshape.120
  23.8 3.0 select_maximum_fusion.2
  26.8 7.8 %fusion.59 = bf16[32,4,16,128]{3,2,1,0:T(8,128)(2,1)S(1)} fusion(bf16[32,4,16,128]{3,2,1,0:T(8,128)(2,1)S(1)} %bitcast.174, bf16[32,1,16,128]{3,2,1,0:T(8,128)(2,1)} %collective-permute-done.1, bf16[32,1,16,128]{3,2,1,0:T(8,128)(2,1)S(1)} %collective-permute-done, f32[32]{0:T(128)} %get-tuple-element.67, f32[32]{0:T(128)} %get-tuple-element.68, ...), kind=kLoop, calls=%fused_computation.140 | loop fusion | flops 21757952 | bytes 13897088 | tf_op jit(solution)/shard_map/convert_element_type | solution.py:154
  37.6 106.7 %all-reduce.2 = (f32[32]{0:T(128)}, f32[2,16,16]{2,1,0:T(8,128)}, f32[2,16,16]{1,2,0:T(8,128)}, f32[32]{0:T(128)}) all-reduce(f32[32]{0:T(128)} %get-tuple-element.93, f32[2,16,16]{2,1,0:T(8,128)} %fusion.215, f32[2,16,16]{1,2,0:T(8,128)} %convolution_bitcast_fusion, ...), channel_id=1, replica_groups=mesh['sample'=32,'space'=16] {'sample','space'}, use_global_device_ids=true, to_apply=%region_2.3 | all-reduce | flops 1088 | bytes 8704 | tf_op jit(solution)/shard_map/psum | solution.py:173
  158.8 1.6 fusion.212
  164.8 1.5 fusion.211
  170.3 1.5 fusion.210
  175.7 1.5 fusion.209
  194.3 1.6 fusion.208
  201.5 1.6 multiply_reduce_fusion.2
  205.8 1.5 multiply_reduce_fusion.3
  214.6 1.5 multiply_bitcast_fusion
  217.5 1.4 reshape.117
  219.0 1.7 convolution_add_fusion.1
  222.0 1.5 fusion.91
  225.0 6.7 %fusion.60 = (f32[32]{0:T(128)S(1)}, f32[32]{0:T(128)S(1)}, f32[32]{0:T(128)}, f32[32]{0:T(128)}, f32[32]{0:T(128)}, /*index=5*/f32[32]{0:T(128)}, f32[32]{0:T(1...) fusion(f32[32,4,16,128]{3,2,1,0:T(8,128)S(1)} %bitcast.164, ...), kind=kLoop, calls=%fused_computation.141 | loop fusion | flops 14155200 | bytes 10488064 | tf_op jit(solution)/shard_map/reduce_sum | solution.py:192
  235.9 4.3 fusion.57
  240.5 2.8 stack.111
  243.3 124.4 %all-reduce.3 = (f32[32,32]{1,0:T(8,128)S(1)}, f32[32,27]{0,1:T(8,128)S(1)}) all-reduce(f32[32,32]{1,0:T(8,128)} %fusion.91, f32[32,27]{0,1:T(8,128)S(1)} %stack.111), channel_id=1, replica_groups=mesh['sample'=32,'space'=16] {'sample'}, use_global_device_ids=true, to_apply=%region_11.12 | all-reduce | flops 1888 | bytes 15104 | tf_op jit(solution)/shard_map/psum | solution.py:16
  367.7 52.4 %all-reduce.4 = (f32[32,32]{1,0:T(8,128)S(1)}, f32[32,27]{0,1:T(8,128)S(1)}) all-reduce(f32[32,32]{1,0:T(8,128)S(1)} %get-tuple-element.73, f32[32,27]{0,1:T(8,128)S(1)} %get-tuple-element.74), channel_id=1, replica_groups=mesh['sample'=32,'space'=16] {'space'}, use_global_device_ids=true, to_apply=%region_12.13 | all-reduce | flops 1888 | bytes 15104 | tf_op jit(solution)/shard_map/psum | solution.py:16
  420.1 5.4 %collective-permute-start.2 = (f32[32,1,16,128]{3,2,1,0:T(8,128)}, f32[32,1,16,128]{3,2,1,0:T(8,128)S(1)}, u32[]{:S(2)}, u32[]{:S(2)}) collective-permute-start(f32[32,1,16,128]{3,2,1,0:T(8,128)} %get-tuple-element.77), channel_id=1, source_target_pairs={{0,1},{1,2},{2,3},{3,4},{4,5},{5,6},{6,7},{7,8},{8,9},{9,10},{10,1... | collective-permute-start | bytes 786440 | tf_op jit(solution)/shard_map/ppermute | solution.py:24
  425.5 1.9 collective-permute-start.3
  427.4 1.6 fusion.5
  431.2 3.9 collective-permute-done.3
  435.2 3.4 select_maximum_fusion
  438.8 25.1 %fusion.94 = bf16[1,32,4,16,128]{4,3,2,1,0:T(8,128)(2,1)} fusion(f32[32,6,18,130]{3,2,1,0:T(8,128)} %select_maximum_fusion, f32[32]{0:T(128)S(1)} %copy-done.23, f32[32]{0:T(128)S(1)} %copy-done.24, f32[32]{0:T(128)S(1)} %copy-done.26, f32[32]{0:T(128)S(1)} %copy-done.27, f32[32,4,16,128]{3,2,1,0:T(8,128)S(1)} %bitcast.168, ...), kind=kLoop, calls=%fused_computation.206 | loop fusion | flops 14680064 | bytes 27266432 | tf_op jit(solution)/shard_map/broadcast_in_dim | solution.py:207
  (181 shorter events, 78.5 us)
Async XLA Ops:
  1.8 22.1 %collective-permute-start = (bf16[32,1,16,128]{3,2,1,0:T(8,128)(2,1)S(1)}, bf16[32,1,16,128]{3,2,1,0:T(8,128)(2,1)S(1)}, u32[]{:S(2)}, u32[]{:S(2)}) collective-permute-start(bf16[32,1,16,128]{3,2,1,0:T(8,128)(2,1)S(1)} %get-tuple-element.79), channel_id=1, source_target_pairs={{0,1},{1,2},{2,3},{3,4},{4,5},{5,6},{6,7},{7,8},{8,9},{9,10},{10,1... | collective-permute-start | bytes 393224 | tf_op jit(solution)/shard_map/ppermute | solution.py:24
  6.8 17.0 %collective-permute-start.1 = (bf16[32,1,16,128]{3,2,1,0:T(8,128)(2,1)S(1)}, bf16[32,1,16,128]{3,2,1,0:T(8,128)(2,1)}, u32[]{:S(2)}, u32[]{:S(2)}) collective-permute-start(bf16[32,1,16,128]{3,2,1,0:T(8,128)(2,1)S(1)} %get-tuple-element.80), channel_id=1, source_target_pairs={{1,0},{2,1},{3,2},{4,3},{5,4},{6,5},{7,6},{8,7},{9,8},{10,9},{11,1... | collective-permute-start | bytes 393224 | tf_op jit(solution)/shard_map/ppermute | solution.py:27
  35.8 186.2 %copy-start.1 = (bf16[8192,32]{0,1:T(8,128)(2,1)}, bf16[8192,32]{0,1:T(8,128)(2,1)S(1)}, u32[]{:S(2)}) copy-start(bf16[8192,32]{0,1:T(8,128)(2,1)S(1)} %get-tuple-element.94) | copy-start | bytes 1572868
  240.3 198.2 %copy-start.17 = (f32[32]{0:T(128)S(1)}, f32[32]{0:T(128)}, u32[]{:S(2)}) copy-start(f32[32]{0:T(128)} %get-tuple-element.61) | copy-start | bytes 388
  240.3 198.2 %copy-start.18 = (f32[32]{0:T(128)S(1)}, f32[32]{0:T(128)}, u32[]{:S(2)}) copy-start(f32[32]{0:T(128)} %get-tuple-element.62) | copy-start | bytes 388
  240.3 198.2 %copy-start.19 = (f32[32]{0:T(128)S(1)}, f32[32]{0:T(128)}, u32[]{:S(2)}) copy-start(f32[32]{0:T(128)} %get-tuple-element.63) | copy-start | bytes 388
  240.3 198.2 %copy-start.20 = (f32[32]{0:T(128)S(1)}, f32[32]{0:T(128)}, u32[]{:S(2)}) copy-start(f32[32]{0:T(128)} %get-tuple-element.64) | copy-start | bytes 388
  240.3 198.3 %copy-start.21 = (f32[32]{0:T(128)S(1)}, f32[32]{0:T(128)}, u32[]{:S(2)}) copy-start(f32[32]{0:T(128)} %get-tuple-element.65) | copy-start | bytes 388
  240.3 198.3 %copy-start.22 = (f32[32]{0:T(128)S(1)}, f32[32]{0:T(128)}, u32[]{:S(2)}) copy-start(f32[32]{0:T(128)} %get-tuple-element.66) | copy-start | bytes 388
  240.3 198.3 %copy-start.23 = (f32[32]{0:T(128)S(1)}, f32[32]{0:T(128)}, u32[]{:S(2)}) copy-start(f32[32]{0:T(128)} %get-tuple-element.67) | copy-start | bytes 388
  240.3 198.3 %copy-start.24 = (f32[32]{0:T(128)S(1)}, f32[32]{0:T(128)}, u32[]{:S(2)}) copy-start(f32[32]{0:T(128)} %get-tuple-element.68) | copy-start | bytes 388
  240.3 198.3 %copy-start.25 = (f32[32]{0:T(128)S(1)}, f32[32]{0:T(128)}, u32[]{:S(2)}) copy-start(f32[32]{0:T(128)} %get-tuple-element.42) | copy-start | bytes 388
  240.3 198.3 %copy-start.26 = (f32[32]{0:T(128)S(1)}, f32[32]{0:T(128)}, u32[]{:S(2)}) copy-start(f32[32]{0:T(128)} %get-tuple-element.43) | copy-start | bytes 388
  240.3 198.3 %copy-start.27 = (f32[32]{0:T(128)S(1)}, f32[32]{0:T(128)}, u32[]{:S(2)}) copy-start(f32[32]{0:T(128)} %get-tuple-element.44) | copy-start | bytes 388
  240.4 198.3 %copy-start.28 = (f32[32]{0:T(128)S(1)}, f32[32]{0:T(128)}, u32[]{:S(2)}) copy-start(f32[32]{0:T(128)} %get-tuple-element.45) | copy-start | bytes 388
  240.4 198.3 %copy-start.29 = (f32[32]{0:T(128)S(1)}, f32[32]{0:T(128)}, u32[]{:S(2)}) copy-start(f32[32]{0:T(128)} %get-tuple-element.46) | copy-start | bytes 388
  240.4 198.3 %copy-start.30 = (f32[32]{0:T(128)S(1)}, f32[32]{0:T(128)}, u32[]{:S(2)}) copy-start(f32[32]{0:T(128)} %get-tuple-element.47) | copy-start | bytes 388
  240.4 198.3 %copy-start.31 = (f32[32]{0:T(128)S(1)}, f32[32]{0:T(128)}, u32[]{:S(2)}) copy-start(f32[32]{0:T(128)} %get-tuple-element.48) | copy-start | bytes 388
  240.4 198.3 %copy-start.32 = (f32[32]{0:T(128)S(1)}, f32[32]{0:T(128)}, u32[]{:S(2)}) copy-start(f32[32]{0:T(128)} %get-tuple-element.49) | copy-start | bytes 388
  240.4 198.3 %copy-start.33 = (f32[32]{0:T(128)S(1)}, f32[32]{0:T(128)}, u32[]{:S(2)}) copy-start(f32[32]{0:T(128)} %get-tuple-element.50) | copy-start | bytes 388
  240.4 198.3 %copy-start.34 = (f32[32]{0:T(128)S(1)}, f32[32]{0:T(128)}, u32[]{:S(2)}) copy-start(f32[32]{0:T(128)} %get-tuple-element.51) | copy-start | bytes 388
  240.4 198.3 %copy-start.35 = (f32[32]{0:T(128)S(1)}, f32[32]{0:T(128)}, u32[]{:S(2)}) copy-start(f32[32]{0:T(128)} %get-tuple-element.52) | copy-start | bytes 388
  240.4 198.3 %copy-start.36 = (f32[32]{0:T(128)S(1)}, f32[32]{0:T(128)}, u32[]{:S(2)}) copy-start(f32[32]{0:T(128)} %get-tuple-element.53) | copy-start | bytes 388
  240.4 198.3 %copy-start.37 = (f32[32]{0:T(128)S(1)}, f32[32]{0:T(128)}, u32[]{:S(2)}) copy-start(f32[32]{0:T(128)} %get-tuple-element.54) | copy-start | bytes 388
  240.5 198.3 %copy-start.38 = (f32[32]{0:T(128)S(1)}, f32[32]{0:T(128)}, u32[]{:S(2)}) copy-start(f32[32]{0:T(128)} %get-tuple-element.55) | copy-start | bytes 388
  240.5 198.3 %copy-start.39 = (f32[32]{0:T(128)S(1)}, f32[32]{0:T(128)}, u32[]{:S(2)}) copy-start(f32[32]{0:T(128)} %get-tuple-element.56) | copy-start | bytes 388
  240.5 198.3 %copy-start.40 = (f32[32]{0:T(128)S(1)}, f32[32]{0:T(128)}, u32[]{:S(2)}) copy-start(f32[32]{0:T(128)} %get-tuple-element.57) | copy-start | bytes 388
  240.5 198.3 %copy-start.41 = (f32[32]{0:T(128)S(1)}, f32[32]{0:T(128)}, u32[]{:S(2)}) copy-start(f32[32]{0:T(128)} %get-tuple-element.58) | copy-start | bytes 388
  240.5 198.3 %copy-start.42 = (f32[32]{0:T(128)S(1)}, f32[32]{0:T(128)}, u32[]{:S(2)}) copy-start(f32[32]{0:T(128)} %get-tuple-element.59) | copy-start | bytes 388
  240.5 198.3 %copy-start.43 = (f32[32]{0:T(128)S(1)}, f32[32]{0:T(128)}, u32[]{:S(2)}) copy-start(f32[32]{0:T(128)} %get-tuple-element.60) | copy-start | bytes 388
  420.1 11.1 %collective-permute-start.2 = (f32[32,1,16,128]{3,2,1,0:T(8,128)}, f32[32,1,16,128]{3,2,1,0:T(8,128)S(1)}, u32[]{:S(2)}, u32[]{:S(2)}) collective-permute-start(f32[32,1,16,128]{3,2,1,0:T(8,128)} %get-tuple-element.77), channel_id=1, source_target_pairs={{0,1},{1,2},{2,3},{3,4},{4,5},{5,6},{6,7},{7,8},{8,9},{9,10},{10,1... | collective-permute-start | bytes 786440 | tf_op jit(solution)/shard_map/ppermute | solution.py:24
  425.5 9.7 %collective-permute-start.3 = (f32[32,1,16,128]{3,2,1,0:T(8,128)}, f32[32,1,16,128]{3,2,1,0:T(8,128)S(1)}, u32[]{:S(2)}, u32[]{:S(2)}) collective-permute-start(f32[32,1,16,128]{3,2,1,0:T(8,128)} %get-tuple-element.78), channel_id=1, source_target_pairs={{1,0},{2,1},{3,2},{4,3},{5,4},{6,5},{7,6},{8,7},{9,8},{10,9},{11,1... | collective-permute-start | bytes 786440 | tf_op jit(solution)/shard_map/ppermute | solution.py:27
  (17 other events, 117.0 us)
